TPU v7x, 32 devices: a whole 2x2x4 slice. The times are simulated.
32 devices in a mesh: row: 8 (over y, x, core), col: 4 (over z).
Axes of the slice: x: 2, y: 2, z: 4, core: 2. Of those that a mesh axis runs over, the one named last changes fastest.
Arguments:
- trial_vectors: bfloat16 [6144, 256], P(('row', 'col')), may hold values from -6 to 6
- h_blocks: bfloat16 [4, 8, 12, 64, 8, 128], P('col', None, None, None, 'row'), may hold values from -0.1875 to 0.1875
- block_col: int32 [4, 8, 12, 8, 2], P('col', 'row'), may hold values from 0 to 2
- block_count: int32 [4, 8, 12, 8], P('col', 'row'), may hold values from 0 to 2, as said below
- center: float32 [1], replicated, may hold values from -0.5 to 0.5
- half_width: float32 [1], replicated, may hold values from 1.5 to 2.5
Outputs:
- filtered: float32 [6144, 256], P(('row', 'col'))
Inputs may be any that keep to these rules, and one draw needn't show every extreme that they name: Only the first block_count slots of a block row and source domain hold blocks. In every column group one row domain has all 2 slots used in every block row for every source domain.
All inputs are finite; a program needn't handle non-finite values.
Results may differ from a plain program's by a relative error of at most 0.019.
Values may be sent and summed in bfloat16 or wider, within the bound.
No kernel may reach another device: no remote copies, remote signals or barrier semaphores. Data moves between devices by JAX's collectives and lax.ppermute only.
A program may use at most 64 MiB of HBM per device.

v0:
```python
import jax
import jax.numpy as jnp
from jax import lax
from jax.sharding import PartitionSpec as P

BLOCK = 64
VECTORS = 256
PER = 2
DEGREE = 6
BLOCK_ROWS = 3


def body(trial_vectors, h_blocks, block_col, block_count, center, half_width):
    arrived = lax.all_to_all(h_blocks, "row", split_axis=1, concat_axis=4, tiled=True)
    row_count = lax.axis_size("row")
    col_count = lax.axis_size("col")
    domain = BLOCK_ROWS * col_count
    filled = (
        lax.broadcasted_iota(jnp.int32, (domain, row_count, PER), 2) < block_count[0, 0][:, :, None]
    )
    shaped = arrived[0, 0].reshape(domain, BLOCK, row_count, PER, BLOCK)
    blocks = jnp.where(filled[:, None, :, :, None], shaped, jnp.zeros((), jnp.bfloat16))
    blocks = blocks.reshape(col_count, BLOCK_ROWS, BLOCK, row_count * PER * BLOCK)
    sources = lax.broadcasted_iota(jnp.int32, (domain, row_count, PER), 1)
    columns = (sources * BLOCK_ROWS + block_col[0, 0]).reshape(
        col_count, BLOCK_ROWS, row_count * PER
    )
    centre_value = center[0]
    half_value = half_width[0]

    def operator(current):
        gathered = lax.all_gather(current, "row", axis=0, tiled=True).reshape(
            row_count * BLOCK_ROWS, BLOCK, VECTORS
        )

        def group_rows(entries):
            group_blocks, group_columns = entries
            picked = gathered[group_columns].reshape(BLOCK_ROWS, row_count * PER * BLOCK, VECTORS)
            return jnp.einsum(
                "rak,rkv->rav", group_blocks, picked, preferred_element_type=jnp.float32
            )

        partial_value = lax.map(group_rows, (blocks, columns)).reshape(domain * BLOCK, VECTORS)
        owned = lax.psum_scatter(
            partial_value.astype(jnp.bfloat16), "col", scatter_dimension=0, tiled=True
        ).astype(jnp.float32)
        return owned

    previous = trial_vectors.astype(jnp.float32)
    current = (operator(trial_vectors) - centre_value * previous) / half_value
    for degree_step in range(DEGREE - 1):
        product = operator(current.astype(jnp.bfloat16))
        following = 2.0 * (product - centre_value * current) / half_value - previous
        previous, current = (current, following)
    return current


def solution(mesh):
    in_specs = (
        P(("row", "col"), None),
        P("col", None, None, None, "row", None),
        P("col", "row", None, None, None),
        P("col", "row", None, None),
        P(),
        P(),
    )
    out_specs = P(("row", "col"), None)
    return jax.shard_map(body, mesh=mesh, in_specs=in_specs, out_specs=out_specs, check_vma=False)
```

profile of v0, /device:TPU:0, one launch (start us, length us, event | category | flops | bytes accessed | tf_op | source)
XLA Modules:
  0.0 303.4 jit_solution(4536157744505953639)
XLA Ops:
  6.5 5.3 %all-to-all-start = ((bf16[1,8,12,64,1,128]{5,3,4,2,0,1:T(8,128)(2,1)}), bf16[1,8,12,64,1,128]{5,3,4,2,0,1:T(8,128)(2,1)S(1)}, u32[]{:S(2)}, u32[]{:S(2)}) async-start(bf16[1,8,12,64,1,128]{5,3,4,2,0,1:T(8,128)(2,1)} %bitcast.176), calls=%async_computation | async-start | bytes 3145728 | tf_op jit(solution)/shard_map/all_to_all | solution.py:14
  12.9 26.2 %all_gather.18 = bf16[1536,256]{1,0:T(8,128)(2,1)} all-gather(bf16[192,256]{1,0:T(8,128)(2,1)S(1)} %copy-done), channel_id=1, replica_groups=mesh['row'=8,'col'=4] {'row'}, dimensions={0}, use_global_device_ids=true | all-gather | bytes 884736 | tf_op jit(solution)/shard_map/all_gather | solution.py:32
  39.1 2.4 copy.27
  41.5 2.5 reshape_squeeze.3
  45.0 11.8 %while.60 = (s32[]{:T(128)}, bf16[4,3,64,256]{3,2,1,0:T(8,128)(2,1)}, bf16[4,3,64,1024]{3,2,1,0:T(8,128)(2,1)S(1)}, s32[4,3,16]{2,0,1:T(4,128)S(1)}, bf16[24,64,256]{2,1,0:T(8,128)(2,1)}, /*index=5*/s32[]{:T(128)}) while((s32[]{:T(128)}, bf16[4,3,64,256]{3,2,1,0:T(8,128)(2,1)}, bf16[4,3,64,1024]{3,2,1,0:T(8,128)(2,1)S(1)}, ...), condition=%wide.region_1.2_spmd, body=%wide.region_0.1_spmd.sunk | while | flops 100664464 | bytes 5314761 | solution.py:43
  45.1 1.8 gather_fusion
  58.1 19.9 %reduce-scatter.7.cloned.1.call-done = bf16[192,256]{1,0:T(8,128)(2,1)} async-done(((bf16[768,256]{1,0:T(8,128)(2,1)}), bf16[192,256]{1,0:T(8,128)(2,1)}) %reduce-scatter.7.cloned.1.call-update) | async-done | bytes 98320 | tf_op jit(solution)/shard_map/reduce_scatter | solution.py:44
  78.9 11.4 %all_gather.19 = bf16[1536,256]{1,0:T(8,128)(2,1)} all-gather(bf16[192,256]{1,0:T(8,128)(2,1)S(1)} %fusion.33), channel_id=1, replica_groups=mesh['row'=8,'col'=4] {'row'}, dimensions={0}, use_global_device_ids=true | all-gather | bytes 884736 | tf_op jit(solution)/shard_map/all_gather | solution.py:32
  91.1 11.8 %while.61 = (s32[]{:T(128)}, bf16[4,3,64,256]{3,2,1,0:T(8,128)(2,1)}, bf16[4,3,64,1024]{3,2,1,0:T(8,128)(2,1)S(1)}, s32[4,3,16]{2,0,1:T(4,128)S(1)}, bf16[24,64,256]{2,1,0:T(8,128)(2,1)}, /*index=5*/s32[]{:T(128)}) while((s32[]{:T(128)}, bf16[4,3,64,256]{3,2,1,0:T(8,128)(2,1)}, bf16[4,3,64,1024]{3,2,1,0:T(8,128)(2,1)S(1)}, ...), condition=%wide.region_4.5_spmd, body=%wide.region_3.4_spmd.sunk | while | flops 100664464 | bytes 5314761 | solution.py:43
  94.1 1.8 gather_fusion.1
  102.9 18.2 %reduce-scatter.9.cloned.1.call-done = bf16[192,256]{1,0:T(8,128)(2,1)} async-done(((bf16[768,256]{1,0:T(8,128)(2,1)}), bf16[192,256]{1,0:T(8,128)(2,1)}) %reduce-scatter.9.cloned.1.call-update) | async-done | bytes 98320 | tf_op jit(solution)/shard_map/reduce_scatter | solution.py:44
  122.1 11.4 %all_gather.20 = bf16[1536,256]{1,0:T(8,128)(2,1)} all-gather(bf16[192,256]{1,0:T(8,128)(2,1)S(1)} %fusion.34), channel_id=1, replica_groups=mesh['row'=8,'col'=4] {'row'}, dimensions={0}, use_global_device_ids=true | all-gather | bytes 884736 | tf_op jit(solution)/shard_map/all_gather | solution.py:32
  134.3 11.8 %while.62 = (s32[]{:T(128)}, bf16[4,3,64,256]{3,2,1,0:T(8,128)(2,1)}, bf16[4,3,64,1024]{3,2,1,0:T(8,128)(2,1)S(1)}, s32[4,3,16]{2,0,1:T(4,128)S(1)}, bf16[24,64,256]{2,1,0:T(8,128)(2,1)}, /*index=5*/s32[]{:T(128)}) while((s32[]{:T(128)}, bf16[4,3,64,256]{3,2,1,0:T(8,128)(2,1)}, bf16[4,3,64,1024]{3,2,1,0:T(8,128)(2,1)S(1)}, ...), condition=%wide.region_7.8_spmd, body=%wide.region_6.7_spmd.sunk | while | flops 100664464 | bytes 5314761 | solution.py:43
  146.1 18.3 %reduce-scatter.11.cloned.1.call-done = bf16[192,256]{1,0:T(8,128)(2,1)} async-done(((bf16[768,256]{1,0:T(8,128)(2,1)}), bf16[192,256]{1,0:T(8,128)(2,1)}) %reduce-scatter.11.cloned.1.call-update) | async-done | bytes 98320 | tf_op jit(solution)/shard_map/reduce_scatter | solution.py:44
  165.4 11.4 %all_gather.21 = bf16[1536,256]{1,0:T(8,128)(2,1)} all-gather(bf16[192,256]{1,0:T(8,128)(2,1)S(1)} %get-tuple-element.325), channel_id=1, replica_groups=mesh['row'=8,'col'=4] {'row'}, dimensions={0}, use_global_device_ids=true | all-gather | bytes 884736 | tf_op jit(solution)/shard_map/all_gather | solution.py:32
  177.6 11.8 %while.63 = (s32[]{:T(128)}, bf16[4,3,64,256]{3,2,1,0:T(8,128)(2,1)}, bf16[4,3,64,1024]{3,2,1,0:T(8,128)(2,1)S(1)}, s32[4,3,16]{2,0,1:T(4,128)S(1)}, bf16[24,64,256]{2,1,0:T(8,128)(2,1)}, /*index=5*/s32[]{:T(128)}) while((s32[]{:T(128)}, bf16[4,3,64,256]{3,2,1,0:T(8,128)(2,1)}, bf16[4,3,64,1024]{3,2,1,0:T(8,128)(2,1)S(1)}, ...), condition=%wide.region_10.11_spmd, body=%wide.region_9.10_spmd.sunk | while | flops 100664464 | bytes 5314761 | solution.py:43
  183.6 1.8 gather_fusion.3
  189.4 18.3 %reduce-scatter.13.cloned.1.call-done = bf16[192,256]{1,0:T(8,128)(2,1)} async-done(((bf16[768,256]{1,0:T(8,128)(2,1)}), bf16[192,256]{1,0:T(8,128)(2,1)}) %reduce-scatter.13.cloned.1.call-update) | async-done | bytes 98320 | tf_op jit(solution)/shard_map/reduce_scatter | solution.py:44
  209.4 11.4 %all_gather.22 = bf16[1536,256]{1,0:T(8,128)(2,1)} all-gather(bf16[192,256]{1,0:T(8,128)(2,1)S(1)} %get-tuple-element.323), channel_id=1, replica_groups=mesh['row'=8,'col'=4] {'row'}, dimensions={0}, use_global_device_ids=true | all-gather | bytes 884736 | tf_op jit(solution)/shard_map/all_gather | solution.py:32
  221.6 11.8 %while.64 = (s32[]{:T(128)}, bf16[4,3,64,256]{3,2,1,0:T(8,128)(2,1)}, bf16[4,3,64,1024]{3,2,1,0:T(8,128)(2,1)S(1)}, s32[4,3,16]{2,0,1:T(4,128)S(1)}, bf16[24,64,256]{2,1,0:T(8,128)(2,1)}, /*index=5*/s32[]{:T(128)}) while((s32[]{:T(128)}, bf16[4,3,64,256]{3,2,1,0:T(8,128)(2,1)}, bf16[4,3,64,1024]{3,2,1,0:T(8,128)(2,1)S(1)}, ...), condition=%wide.region_13.14_spmd, body=%wide.region_12.13_spmd.sunk | while | flops 100664464 | bytes 5314761 | solution.py:43
  233.4 18.3 %reduce-scatter.15.cloned.1.call-done = bf16[192,256]{1,0:T(8,128)(2,1)} async-done(((bf16[768,256]{1,0:T(8,128)(2,1)}), bf16[192,256]{1,0:T(8,128)(2,1)}) %reduce-scatter.15.cloned.1.call-update) | async-done | bytes 98320 | tf_op jit(solution)/shard_map/reduce_scatter | solution.py:44
  252.6 11.4 %all_gather.23 = bf16[1536,256]{1,0:T(8,128)(2,1)} all-gather(bf16[192,256]{1,0:T(8,128)(2,1)S(1)} %fusion.32), channel_id=1, replica_groups=mesh['row'=8,'col'=4] {'row'}, dimensions={0}, use_global_device_ids=true | all-gather | bytes 884736 | tf_op jit(solution)/shard_map/all_gather | solution.py:32
  264.8 11.8 %while.65 = (s32[]{:T(128)}, bf16[4,3,64,256]{3,2,1,0:T(8,128)(2,1)}, bf16[4,3,64,1024]{3,2,1,0:T(8,128)(2,1)S(1)}, s32[4,3,16]{2,0,1:T(4,128)S(1)}, bf16[24,64,256]{2,1,0:T(8,128)(2,1)}, /*index=5*/s32[]{:T(128)}) while((s32[]{:T(128)}, bf16[4,3,64,256]{3,2,1,0:T(8,128)(2,1)}, bf16[4,3,64,1024]{3,2,1,0:T(8,128)(2,1)S(1)}, ...), condition=%wide.region_16.17_spmd, body=%wide.region_15.16_spmd.sunk | while | flops 100664464 | bytes 5314761 | solution.py:43
  276.6 18.3 %reduce-scatter.17.cloned.1.call-done = bf16[192,256]{1,0:T(8,128)(2,1)} async-done(((bf16[768,256]{1,0:T(8,128)(2,1)}), bf16[192,256]{1,0:T(8,128)(2,1)}) %reduce-scatter.17.cloned.1.call-update) | async-done | bytes 98320 | tf_op jit(solution)/shard_map/reduce_scatter | solution.py:44
  (163 shorter events, 78.3 us)
Async XLA Ops:
  6.5 5.4 %copy-start.4 = (s32[1,1,12,8]{2,3,1,0:T(8,128)S(1)}, s32[1,1,12,8]{2,3,1,0:T(8,128)}, u32[]{:S(2)}) copy-start(s32[1,1,12,8]{2,3,1,0:T(8,128)} %param.21) | copy-start | bytes 1156
  6.5 5.9 %copy-start.3 = (s32[1,1,12,8,2]{2,4,3,1,0:T(2,128)S(1)}, s32[1,1,12,8,2]{2,4,3,1,0:T(2,128)}, u32[]{:S(2)}) copy-start(s32[1,1,12,8,2]{2,4,3,1,0:T(2,128)} %param.20) | copy-start | bytes 2308
  6.5 6.3 %copy-start = (bf16[192,256]{1,0:T(8,128)(2,1)S(1)}, bf16[192,256]{1,0:T(8,128)(2,1)}, u32[]{:S(2)}) copy-start(bf16[192,256]{1,0:T(8,128)(2,1)} %param.18) | copy-start | bytes 294916
  6.5 32.6 %all-to-all-start = ((bf16[1,8,12,64,1,128]{5,3,4,2,0,1:T(8,128)(2,1)}), bf16[1,8,12,64,1,128]{5,3,4,2,0,1:T(8,128)(2,1)S(1)}, u32[]{:S(2)}, u32[]{:S(2)}) async-start(bf16[1,8,12,64,1,128]{5,3,4,2,0,1:T(8,128)(2,1)} %bitcast.176), calls=%async_computation | async-start | bytes 3145728 | tf_op jit(solution)/shard_map/all_to_all | solution.py:14
  11.9 66.1 %reduce-scatter.7.cloned.1.call-start = ((), (), s32[]{:S(2)}) async-start(), calls=%async_computation.7 | async-start | bytes 491520 | tf_op jit(solution)/shard_map/reduce_scatter | solution.py:44
  56.8 64.4 %reduce-scatter.9.cloned.1.call-start = ((), (), s32[]{:S(2)}) async-start(), calls=%async_computation.8 | async-start | bytes 491520 | tf_op jit(solution)/shard_map/reduce_scatter | solution.py:44
  91.1 30.1 %copy-start.2 = (bf16[192,256]{1,0:T(8,128)(2,1)S(1)}, bf16[192,256]{1,0:T(8,128)(2,1)}, u32[]{:S(2)}) copy-start(bf16[192,256]{1,0:T(8,128)(2,1)} %reduce-scatter.7.cloned.1.call-done) | copy-start | bytes 294916
  102.9 61.5 %reduce-scatter.11.cloned.1.call-start = ((), (), s32[]{:S(2)}) async-start(), calls=%async_computation.9 | async-start | bytes 491520 | tf_op jit(solution)/shard_map/reduce_scatter | solution.py:44
  146.1 61.6 %reduce-scatter.13.cloned.1.call-start = ((), (), s32[]{:S(2)}) async-start(), calls=%async_computation.10 | async-start | bytes 491520 | tf_op jit(solution)/shard_map/reduce_scatter | solution.py:44
  189.4 62.3 %reduce-scatter.15.cloned.1.call-start = ((), (), s32[]{:S(2)}) async-start(), calls=%async_computation.11 | async-start | bytes 491520 | tf_op jit(solution)/shard_map/reduce_scatter | solution.py:44
  221.6 30.1 %copy-start.1 = (f32[192,256]{1,0:T(8,128)S(1)}, f32[192,256]{1,0:T(8,128)}, u32[]{:S(2)}) copy-start(f32[192,256]{1,0:T(8,128)} %get-tuple-element.324) | copy-start | bytes 589828
  233.4 61.5 %reduce-scatter.17.cloned.1.call-start = ((), (), s32[]{:S(2)}) async-start(), calls=%async_computation.12 | async-start | bytes 491520 | tf_op jit(solution)/shard_map/reduce_scatter | solution.py:44
Sparse Core Ops, SparseCore 0:
  56.9 21.0 reduce-scatter.6
  103.0 18.1 reduce-scatter.8
  146.2 18.1 reduce-scatter.10
  189.5 18.1 reduce-scatter.12
  233.5 18.1 reduce-scatter.14
  276.7 18.1 reduce-scatter.16
where the time goes:
time: 305 us; the launch traced here: 303 us
  waiting for transfers between devices  111 us (36%)
  blocking collectives  83.1 us (27%)
  local copies, waits for them, and re-layouts  55.5 us (18%)
  matrix products  24.4 us (8%)
  between operations  14.9 us (5%)
  other arithmetic  8.43 us (3%)
  starting transfers between devices  5.57 us (2%)
    reduce_scatter x6, waiting for transfers between devices, operator(): lax.psum_scatter(partial_value.astype(jnp.bfloat16), 'col', scatter_dimen...  111 us
    all_gather x6, blocking collectives, operator(): lax.all_gather(current, 'row', axis=0, tiled=True)  83.1 us
    gather x24, local copies, waits for them, and re-layouts, group_rows(): gathered[group_columns]  43 us
    dot_general x24, matrix products, group_rows(): jnp.einsum('rak,rkv->rav', group_blocks, picked, preferred_element_type=j...  24.4 us
  transfers between devices with their start and end apart: 7, of which 6 were waited for; matrix products, arithmetic and copies ran while one was open for 0% of the time, Pallas kernels for 0%

commit v1 on v0

--- a/solution.py
+++ b/solution.py
@@ -8,6 +8,24 @@
 PER = 2
 DEGREE = 6
 BLOCK_ROWS = 3
+
+
+def gather_around(shard, axis, dim):
+    ways, here, step = (lax.axis_size(axis), lax.axis_index(axis), shard.shape[dim])
+    lengths = [n * ways if d == dim else n for d, n in enumerate(shard.shape)]
+    full = lax.dynamic_update_slice_in_dim(
+        jnp.zeros(lengths, shard.dtype), shard, here * step, axis=dim
+    )
+    going_up = going_down = shard
+    for far in range(1, ways // 2 + 1):
+        going_up = lax.ppermute(going_up, axis, [(d, (d + 1) % ways) for d in range(ways)])
+        full = lax.dynamic_update_slice_in_dim(full, going_up, (here - far) % ways * step, axis=dim)
+        if 2 * far < ways:
+            going_down = lax.ppermute(going_down, axis, [(d, (d - 1) % ways) for d in range(ways)])
+            full = lax.dynamic_update_slice_in_dim(
+                full, going_down, (here + far) % ways * step, axis=dim
+            )
+    return full
 
 
 def body(trial_vectors, h_blocks, block_col, block_count, center, half_width):
@@ -29,9 +47,7 @@
     half_value = half_width[0]
 
     def operator(current):
-        gathered = lax.all_gather(current, "row", axis=0, tiled=True).reshape(
-            row_count * BLOCK_ROWS, BLOCK, VECTORS
-        )
+        gathered = gather_around(current, "row", 0).reshape(row_count * BLOCK_ROWS, BLOCK, VECTORS)
 
         def group_rows(entries):
             group_blocks, group_columns = entries

time: 305 us -> 371 us (1.22)
  blocking collectives: 83.1 us -> 0 us
  waiting for transfers between devices: 111 us -> 183 us
  starting transfers between devices: 5.57 us -> 53.1 us
  local copies, waits for them, and re-layouts: 55.5 us -> 83.7 us
    all_gather x6 -> x0, blocking collectives: 83.1 us -> none  [operator(): lax.all_gather(current, 'row', axis=0, tiled=True)]
    ppermute x0 -> x42, waiting for transfers between devices: none -> 66.3 us  [the longest x24 62.2 us: gather_around(): lax.ppermute(going_up, axis, [(d, (d + 1) % ways) for d in range(ways)])]
    ppermute x0 -> x42, starting transfers between devices: none -> 49.1 us  [the longest x18 48.2 us: gather_around(): lax.ppermute(going_down, axis, [(d, (d - 1) % ways) for d in range(ways)])]
    dynamic_update_slice x0 -> x43, local copies, waits for them, and re-layouts: none -> 23.1 us  [the longest x24 12.8 us: gather_around(): lax.dynamic_update_slice_in_dim(full, going_up, (here - far) % ways * ste...]
    dynamic_update_slice x0 -> x5, other arithmetic: none -> 7.53 us  [gather_around(): lax.dynamic_update_slice_in_dim(jnp.zeros(lengths, shard.dtype), shard, h...]
    convert_element_type x5 -> x0, other arithmetic: 5.64 us -> none  [body(): product = operator(current.astype(jnp.bfloat16))]
    reduce_scatter x6, waiting for transfers between devices: 111 us -> 116 us  [operator(): lax.psum_scatter(partial_value.astype(jnp.bfloat16), 'col', scatter_dimen...]
    another operation x6 -> x12, local copies, waits for them, and re-layouts: 4.67 us -> 9.56 us
  transfers between devices with their start and end apart: 7 -> 49, of which waited for: 6 -> 38; matrix products, arithmetic and copies ran while one was open for 0% -> 6% of each run, Pallas kernels for 0% -> 0%
where the time goes in v1:
time: 371 us; the launch traced here: 370 us
  waiting for transfers between devices  183 us (49%)
  local copies, waits for them, and re-layouts  83.7 us (23%)
  starting transfers between devices  53.1 us (14%)
  matrix products  24.5 us (7%)
  between operations  15.1 us (4%)
  other arithmetic  10.3 us (3%)
    reduce_scatter x6, waiting for transfers between devices, operator(): lax.psum_scatter(partial_value.astype(jnp.bfloat16), 'col', scatter_dimen...  116 us
    ppermute x24, waiting for transfers between devices, gather_around(): lax.ppermute(going_up, axis, [(d, (d + 1) % ways) for d in range(ways)])  62.2 us
    ppermute x18, starting transfers between devices, gather_around(): lax.ppermute(going_down, axis, [(d, (d - 1) % ways) for d in range(ways)])  48.2 us
    gather x24, local copies, waits for them, and re-layouts, group_rows(): gathered[group_columns]  43 us
    dot_general x24, matrix products, group_rows(): jnp.einsum('rak,rkv->rav', group_blocks, picked, preferred_element_type=j...  24.5 us
    dynamic_update_slice x24, local copies, waits for them, and re-layouts, gather_around(): lax.dynamic_update_slice_in_dim(full, going_up, (here - far) % ways * ste...  12.8 us
    dynamic_update_slice x18, local copies, waits for them, and re-layouts, gather_around(): lax.dynamic_update_slice_in_dim(full, going_down, (here + far) % ways * s...  9.65 us
    another operation x12, local copies, waits for them, and re-layouts  9.56 us
  transfers between devices with their start and end apart: 49, of which 38 were waited for; matrix products, arithmetic and copies ran while one was open for 6% of the time, Pallas kernels for 0%

profile of v1, /device:TPU:0, one launch (start us, length us, event | category | flops | bytes accessed | tf_op | source)
XLA Modules:
  0.0 369.5 jit_solution(1182048212100793228)
XLA Ops:
  7.0 2.9 collective-permute-start.1
  9.9 3.7 %all-to-all-start = ((bf16[1,8,12,64,1,128]{5,3,4,2,0,1:T(8,128)(2,1)}), bf16[1,8,12,64,1,128]{5,3,4,2,0,1:T(8,128)(2,1)S(1)}, u32[]{:S(2)}, u32[]{:S(2)}) async-start(bf16[1,8,12,64,1,128]{5,3,4,2,0,1:T(8,128)(2,1)} %bitcast.171), calls=%async_computation | async-start | bytes 3145728 | tf_op jit(solution)/shard_map/all_to_all | solution.py:32
  20.3 15.9 %collective-permute-done.2 = bf16[192,256]{1,0:T(8,128)(2,1)S(1)} collective-permute-done((bf16[192,256]{1,0:T(8,128)(2,1)S(1)}, bf16[192,256]{1,0:T(8,128)(2,1)S(1)}, u32[]{:S(2)}, u32[]{:S(2)}) %collective-permute-start.2) | collective-permute-done | bytes 98336 | tf_op jit(solution)/shard_map/ppermute | solution.py:21
  43.3 3.7 collective-permute-done.6
  53.5 11.8 %while.60 = (s32[]{:T(128)}, bf16[4,3,64,256]{3,2,1,0:T(8,128)(2,1)}, bf16[4,3,64,1024]{3,2,1,0:T(8,128)(2,1)S(1)}, s32[4,3,16]{2,0,1:T(4,128)S(1)}, bf16[24,64,256]{2,1,0:T(8,128)(2,1)}, /*index=5*/s32[]{:T(128)}) while((s32[]{:T(128)}, bf16[4,3,64,256]{3,2,1,0:T(8,128)(2,1)}, bf16[4,3,64,1024]{3,2,1,0:T(8,128)(2,1)S(1)}, ...), condition=%wide.region_1.2_spmd, body=%wide.region_0.1_spmd.sunk | while | flops 100664464 | bytes 5314761 | solution.py:59
  66.6 19.8 %reduce-scatter.7.cloned.1.call-done = bf16[192,256]{1,0:T(8,128)(2,1)} async-done(((bf16[768,256]{1,0:T(8,128)(2,1)}), bf16[192,256]{1,0:T(8,128)(2,1)}) %reduce-scatter.7.cloned.1.call-update) | async-done | bytes 98320 | tf_op jit(solution)/shard_map/reduce_scatter | solution.py:60
  99.6 2.8 collective-permute-start.12
  106.1 2.8 collective-permute-done.13
  110.3 11.8 %while.61 = (s32[]{:T(128)}, bf16[4,3,64,256]{3,2,1,0:T(8,128)(2,1)}, bf16[4,3,64,1024]{3,2,1,0:T(8,128)(2,1)S(1)}, s32[4,3,16]{2,0,1:T(4,128)S(1)}, bf16[24,64,256]{2,1,0:T(8,128)(2,1)}, /*index=5*/s32[]{:T(128)}) while((s32[]{:T(128)}, bf16[4,3,64,256]{3,2,1,0:T(8,128)(2,1)}, bf16[4,3,64,1024]{3,2,1,0:T(8,128)(2,1)S(1)}, ...), condition=%wide.region_4.5_spmd, body=%wide.region_3.4_spmd.sunk | while | flops 100664464 | bytes 5314761 | solution.py:59
  122.2 19.5 %reduce-scatter.9.cloned.1.call-done = bf16[192,256]{1,0:T(8,128)(2,1)} async-done(((bf16[768,256]{1,0:T(8,128)(2,1)}), bf16[192,256]{1,0:T(8,128)(2,1)}) %reduce-scatter.9.cloned.1.call-update) | async-done | bytes 98320 | tf_op jit(solution)/shard_map/reduce_scatter | solution.py:60
  154.9 2.8 collective-permute-start.19
  165.6 11.8 %while.62 = (s32[]{:T(128)}, bf16[4,3,64,256]{3,2,1,0:T(8,128)(2,1)}, bf16[4,3,64,1024]{3,2,1,0:T(8,128)(2,1)S(1)}, s32[4,3,16]{2,0,1:T(4,128)S(1)}, bf16[24,64,256]{2,1,0:T(8,128)(2,1)}, /*index=5*/s32[]{:T(128)}) while((s32[]{:T(128)}, bf16[4,3,64,256]{3,2,1,0:T(8,128)(2,1)}, bf16[4,3,64,1024]{3,2,1,0:T(8,128)(2,1)S(1)}, ...), condition=%wide.region_7.8_spmd, body=%wide.region_6.7_spmd.sunk | while | flops 100664464 | bytes 5314761 | solution.py:59
  177.4 19.6 %reduce-scatter.11.cloned.1.call-done = bf16[192,256]{1,0:T(8,128)(2,1)} async-done(((bf16[768,256]{1,0:T(8,128)(2,1)}), bf16[192,256]{1,0:T(8,128)(2,1)}) %reduce-scatter.11.cloned.1.call-update) | async-done | bytes 98320 | tf_op jit(solution)/shard_map/reduce_scatter | solution.py:60
  210.4 2.8 collective-permute-start.26
  216.8 2.8 collective-permute-done.27
  221.1 11.8 %while.63 = (s32[]{:T(128)}, bf16[4,3,64,256]{3,2,1,0:T(8,128)(2,1)}, bf16[4,3,64,1024]{3,2,1,0:T(8,128)(2,1)S(1)}, s32[4,3,16]{2,0,1:T(4,128)S(1)}, bf16[24,64,256]{2,1,0:T(8,128)(2,1)}, /*index=5*/s32[]{:T(128)}) while((s32[]{:T(128)}, bf16[4,3,64,256]{3,2,1,0:T(8,128)(2,1)}, bf16[4,3,64,1024]{3,2,1,0:T(8,128)(2,1)S(1)}, ...), condition=%wide.region_10.11_spmd, body=%wide.region_9.10_spmd.sunk | while | flops 100664464 | bytes 5314761 | solution.py:59
  232.9 19.5 %reduce-scatter.13.cloned.1.call-done = bf16[192,256]{1,0:T(8,128)(2,1)} async-done(((bf16[768,256]{1,0:T(8,128)(2,1)}), bf16[192,256]{1,0:T(8,128)(2,1)}) %reduce-scatter.13.cloned.1.call-update) | async-done | bytes 98320 | tf_op jit(solution)/shard_map/reduce_scatter | solution.py:60
  272.2 2.8 collective-permute-done.34
  276.5 11.8 %while.64 = (s32[]{:T(128)}, bf16[4,3,64,256]{3,2,1,0:T(8,128)(2,1)}, bf16[4,3,64,1024]{3,2,1,0:T(8,128)(2,1)S(1)}, s32[4,3,16]{2,0,1:T(4,128)S(1)}, bf16[24,64,256]{2,1,0:T(8,128)(2,1)}, /*index=5*/s32[]{:T(128)}) while((s32[]{:T(128)}, bf16[4,3,64,256]{3,2,1,0:T(8,128)(2,1)}, bf16[4,3,64,1024]{3,2,1,0:T(8,128)(2,1)S(1)}, ...), condition=%wide.region_13.14_spmd, body=%wide.region_12.13_spmd.sunk | while | flops 100664464 | bytes 5314761 | solution.py:59
  288.3 19.6 %reduce-scatter.15.cloned.1.call-done = bf16[192,256]{1,0:T(8,128)(2,1)} async-done(((bf16[768,256]{1,0:T(8,128)(2,1)}), bf16[192,256]{1,0:T(8,128)(2,1)}) %reduce-scatter.15.cloned.1.call-update) | async-done | bytes 98320 | tf_op jit(solution)/shard_map/reduce_scatter | solution.py:60
  321.9 3.1 collective-permute-done.39
  325.0 4.8 %collective-permute-done.41 = bf16[192,256]{1,0:T(8,128)(2,1)S(1)} collective-permute-done((bf16[192,256]{1,0:T(8,128)(2,1)S(1)}, bf16[192,256]{1,0:T(8,128)(2,1)S(1)}, u32[]{:S(2)}, u32[]{:S(2)}) %collective-permute-start.41) | collective-permute-done | bytes 98336 | tf_op jit(solution)/shard_map/ppermute | solution.py:21
  330.9 11.8 %while.65 = (s32[]{:T(128)}, bf16[4,3,64,256]{3,2,1,0:T(8,128)(2,1)}, bf16[4,3,64,1024]{3,2,1,0:T(8,128)(2,1)S(1)}, s32[4,3,16]{2,0,1:T(4,128)S(1)}, bf16[24,64,256]{2,1,0:T(8,128)(2,1)}, /*index=5*/s32[]{:T(128)}) while((s32[]{:T(128)}, bf16[4,3,64,256]{3,2,1,0:T(8,128)(2,1)}, bf16[4,3,64,1024]{3,2,1,0:T(8,128)(2,1)S(1)}, ...), condition=%wide.region_16.17_spmd, body=%wide.region_15.16_spmd.sunk | while | flops 100664464 | bytes 5314761 | solution.py:59
  342.7 18.3 %reduce-scatter.17.cloned.1.call-done = bf16[192,256]{1,0:T(8,128)(2,1)} async-done(((bf16[768,256]{1,0:T(8,128)(2,1)}), bf16[192,256]{1,0:T(8,128)(2,1)}) %reduce-scatter.17.cloned.1.call-update) | async-done | bytes 98320 | tf_op jit(solution)/shard_map/reduce_scatter | solution.py:60
  (292 shorter events, 187.0 us)
Async XLA Ops:
  6.5 9.8 %collective-permute-start = (bf16[192,256]{1,0:T(8,128)(2,1)}, bf16[192,256]{1,0:T(8,128)(2,1)S(1)}, u32[]{:S(2)}, u32[]{:S(2)}) collective-permute-start(bf16[192,256]{1,0:T(8,128)(2,1)} %param.18), channel_id=1, source_target_pairs={{0,4},{4,8},{8,12},{12,16},{16,20},{20,24},{24,28},{28,0},{1,5},{5... | collective-permute-start | bytes 294920 | tf_op jit(solution)/shard_map/ppermute | solution.py:21
  7.0 9.6 %collective-permute-start.1 = (bf16[192,256]{1,0:T(8,128)(2,1)}, bf16[192,256]{1,0:T(8,128)(2,1)S(1)}, u32[]{:S(2)}, u32[]{:S(2)}) collective-permute-start(bf16[192,256]{1,0:T(8,128)(2,1)} %param.18), channel_id=1, source_target_pairs={{0,28},{4,0},{8,4},{12,8},{16,12},{20,16},{24,20},{28,24},{1,29},{... | collective-permute-start | bytes 294920 | tf_op jit(solution)/shard_map/ppermute | solution.py:24
  9.9 37.7 %all-to-all-start = ((bf16[1,8,12,64,1,128]{5,3,4,2,0,1:T(8,128)(2,1)}), bf16[1,8,12,64,1,128]{5,3,4,2,0,1:T(8,128)(2,1)S(1)}, u32[]{:S(2)}, u32[]{:S(2)}) async-start(bf16[1,8,12,64,1,128]{5,3,4,2,0,1:T(8,128)(2,1)} %bitcast.171), calls=%async_computation | async-start | bytes 3145728 | tf_op jit(solution)/shard_map/all_to_all | solution.py:32
  13.6 72.8 %reduce-scatter.7.cloned.1.call-start = ((), (), s32[]{:S(2)}) async-start(), calls=%async_computation.7 | async-start | bytes 491520 | tf_op jit(solution)/shard_map/reduce_scatter | solution.py:60
  16.3 19.8 %collective-permute-start.2 = (bf16[192,256]{1,0:T(8,128)(2,1)S(1)}, bf16[192,256]{1,0:T(8,128)(2,1)S(1)}, u32[]{:S(2)}, u32[]{:S(2)}) collective-permute-start(bf16[192,256]{1,0:T(8,128)(2,1)S(1)} %collective-permute-done), channel_id=1, source_target_pairs={{0,4},{4,8},{8,12},{12,16},{16,20},{20,24},{24,28},{28,0},{1,5},{5... | collective-permute-start | bytes 294920 | tf_op jit(solution)/shard_map/ppermute | solution.py:21
  16.6 19.5 %collective-permute-start.3 = (bf16[192,256]{1,0:T(8,128)(2,1)S(1)}, bf16[192,256]{1,0:T(8,128)(2,1)S(1)}, u32[]{:S(2)}, u32[]{:S(2)}) collective-permute-start(bf16[192,256]{1,0:T(8,128)(2,1)S(1)} %collective-permute-done.1), channel_id=1, source_target_pairs={{0,28},{4,0},{8,4},{12,8},{16,12},{20,16},{24,20},{28,24},{1,29},{... | collective-permute-start | bytes 294920 | tf_op jit(solution)/shard_map/ppermute | solution.py:24
  36.1 5.8 %collective-permute-start.4 = (bf16[192,256]{1,0:T(8,128)(2,1)S(1)}, bf16[192,256]{1,0:T(8,128)(2,1)S(1)}, u32[]{:S(2)}, u32[]{:S(2)}) collective-permute-start(bf16[192,256]{1,0:T(8,128)(2,1)S(1)} %collective-permute-done.2), channel_id=1, source_target_pairs={{0,4},{4,8},{8,12},{12,16},{16,20},{20,24},{24,28},{28,0},{1,5},{5... | collective-permute-start | bytes 294920 | tf_op jit(solution)/shard_map/ppermute | solution.py:21
  36.2 6.5 %collective-permute-start.5 = (bf16[192,256]{1,0:T(8,128)(2,1)S(1)}, bf16[192,256]{1,0:T(8,128)(2,1)S(1)}, u32[]{:S(2)}, u32[]{:S(2)}) collective-permute-start(bf16[192,256]{1,0:T(8,128)(2,1)S(1)} %collective-permute-done.3), channel_id=1, source_target_pairs={{0,28},{4,0},{8,4},{12,8},{16,12},{20,16},{24,20},{28,24},{1,29},{... | collective-permute-start | bytes 294920 | tf_op jit(solution)/shard_map/ppermute | solution.py:24
  65.3 76.4 %reduce-scatter.9.cloned.1.call-start = ((), (), s32[]{:S(2)}) async-start(), calls=%async_computation.8 | async-start | bytes 491520 | tf_op jit(solution)/shard_map/reduce_scatter | solution.py:60
  88.9 5.6 %collective-permute-start.8 = (bf16[192,256]{1,0:T(8,128)(2,1)S(1)}, bf16[192,256]{1,0:T(8,128)(2,1)S(1)}, u32[]{:S(2)}, u32[]{:S(2)}) collective-permute-start(bf16[192,256]{1,0:T(8,128)(2,1)S(1)} %get-tuple-element.334), channel_id=1, source_target_pairs={{0,28},{4,0},{8,4},{12,8},{16,12},{20,16},{24,20},{28,24},{1,29},{... | collective-permute-start | bytes 294920 | tf_op jit(solution)/shard_map/ppermute | solution.py:24
  99.6 5.9 %collective-permute-start.12 = (bf16[192,256]{1,0:T(8,128)(2,1)S(1)}, bf16[192,256]{1,0:T(8,128)(2,1)S(1)}, u32[]{:S(2)}, u32[]{:S(2)}) collective-permute-start(bf16[192,256]{1,0:T(8,128)(2,1)S(1)} %collective-permute-done.10), channel_id=1, source_target_pairs={{0,28},{4,0},{8,4},{12,8},{16,12},{20,16},{24,20},{28,24},{1,29},{... | collective-permute-start | bytes 294920 | tf_op jit(solution)/shard_map/ppermute | solution.py:24
  122.1 74.9 %reduce-scatter.11.cloned.1.call-start = ((), (), s32[]{:S(2)}) async-start(), calls=%async_computation.9 | async-start | bytes 491520 | tf_op jit(solution)/shard_map/reduce_scatter | solution.py:60
  144.2 5.6 %collective-permute-start.15 = (bf16[192,256]{1,0:T(8,128)(2,1)S(1)}, bf16[192,256]{1,0:T(8,128)(2,1)S(1)}, u32[]{:S(2)}, u32[]{:S(2)}) collective-permute-start(bf16[192,256]{1,0:T(8,128)(2,1)S(1)} %get-tuple-element.332), channel_id=1, source_target_pairs={{0,28},{4,0},{8,4},{12,8},{16,12},{20,16},{24,20},{28,24},{1,29},{... | collective-permute-start | bytes 294920 | tf_op jit(solution)/shard_map/ppermute | solution.py:24
  154.9 5.8 %collective-permute-start.19 = (bf16[192,256]{1,0:T(8,128)(2,1)S(1)}, bf16[192,256]{1,0:T(8,128)(2,1)S(1)}, u32[]{:S(2)}, u32[]{:S(2)}) collective-permute-start(bf16[192,256]{1,0:T(8,128)(2,1)S(1)} %collective-permute-done.17), channel_id=1, source_target_pairs={{0,28},{4,0},{8,4},{12,8},{16,12},{20,16},{24,20},{28,24},{1,29},{... | collective-permute-start | bytes 294920 | tf_op jit(solution)/shard_map/ppermute | solution.py:24
  177.4 75.0 %reduce-scatter.13.cloned.1.call-start = ((), (), s32[]{:S(2)}) async-start(), calls=%async_computation.10 | async-start | bytes 491520 | tf_op jit(solution)/shard_map/reduce_scatter | solution.py:60
  199.7 5.6 %collective-permute-start.22 = (bf16[192,256]{1,0:T(8,128)(2,1)S(1)}, bf16[192,256]{1,0:T(8,128)(2,1)S(1)}, u32[]{:S(2)}, u32[]{:S(2)}) collective-permute-start(bf16[192,256]{1,0:T(8,128)(2,1)S(1)} %get-tuple-element.329), channel_id=1, source_target_pairs={{0,28},{4,0},{8,4},{12,8},{16,12},{20,16},{24,20},{28,24},{1,29},{... | collective-permute-start | bytes 294920 | tf_op jit(solution)/shard_map/ppermute | solution.py:24
  210.4 5.8 %collective-permute-start.26 = (bf16[192,256]{1,0:T(8,128)(2,1)S(1)}, bf16[192,256]{1,0:T(8,128)(2,1)S(1)}, u32[]{:S(2)}, u32[]{:S(2)}) collective-permute-start(bf16[192,256]{1,0:T(8,128)(2,1)S(1)} %collective-permute-done.24), channel_id=1, source_target_pairs={{0,28},{4,0},{8,4},{12,8},{16,12},{20,16},{24,20},{28,24},{1,29},{... | collective-permute-start | bytes 294920 | tf_op jit(solution)/shard_map/ppermute | solution.py:24
  232.8 75.0 %reduce-scatter.15.cloned.1.call-start = ((), (), s32[]{:S(2)}) async-start(), calls=%async_computation.11 | async-start | bytes 491520 | tf_op jit(solution)/shard_map/reduce_scatter | solution.py:60
  255.1 5.6 %collective-permute-start.29 = (bf16[192,256]{1,0:T(8,128)(2,1)S(1)}, bf16[192,256]{1,0:T(8,128)(2,1)S(1)}, u32[]{:S(2)}, u32[]{:S(2)}) collective-permute-start(bf16[192,256]{1,0:T(8,128)(2,1)S(1)} %get-tuple-element.326), channel_id=1, source_target_pairs={{0,28},{4,0},{8,4},{12,8},{16,12},{20,16},{24,20},{28,24},{1,29},{... | collective-permute-start | bytes 294920 | tf_op jit(solution)/shard_map/ppermute | solution.py:24
  265.8 5.8 %collective-permute-start.33 = (bf16[192,256]{1,0:T(8,128)(2,1)S(1)}, bf16[192,256]{1,0:T(8,128)(2,1)S(1)}, u32[]{:S(2)}, u32[]{:S(2)}) collective-permute-start(bf16[192,256]{1,0:T(8,128)(2,1)S(1)} %collective-permute-done.31), channel_id=1, source_target_pairs={{0,28},{4,0},{8,4},{12,8},{16,12},{20,16},{24,20},{28,24},{1,29},{... | collective-permute-start | bytes 294920 | tf_op jit(solution)/shard_map/ppermute | solution.py:24
  288.3 72.7 %reduce-scatter.17.cloned.1.call-start = ((), (), s32[]{:S(2)}) async-start(), calls=%async_computation.12 | async-start | bytes 491520 | tf_op jit(solution)/shard_map/reduce_scatter | solution.py:60
  313.9 5.2 %collective-permute-start.37 = (bf16[192,256]{1,0:T(8,128)(2,1)S(1)}, bf16[192,256]{1,0:T(8,128)(2,1)S(1)}, u32[]{:S(2)}, u32[]{:S(2)}) collective-permute-start(bf16[192,256]{1,0:T(8,128)(2,1)S(1)} %collective-permute-done.35), channel_id=1, source_target_pairs={{0,4},{4,8},{8,12},{12,16},{16,20},{20,24},{24,28},{28,0},{1,5},{5... | collective-permute-start | bytes 294920 | tf_op jit(solution)/shard_map/ppermute | solution.py:21
  319.1 5.8 %collective-permute-start.39 = (bf16[192,256]{1,0:T(8,128)(2,1)S(1)}, bf16[192,256]{1,0:T(8,128)(2,1)S(1)}, u32[]{:S(2)}, u32[]{:S(2)}) collective-permute-start(bf16[192,256]{1,0:T(8,128)(2,1)S(1)} %collective-permute-done.37), channel_id=1, source_target_pairs={{0,4},{4,8},{8,12},{12,16},{16,20},{20,24},{24,28},{28,0},{1,5},{5... | collective-permute-start | bytes 294920 | tf_op jit(solution)/shard_map/ppermute | solution.py:21
  319.1 5.9 %collective-permute-start.40 = (bf16[192,256]{1,0:T(8,128)(2,1)S(1)}, bf16[192,256]{1,0:T(8,128)(2,1)S(1)}, u32[]{:S(2)}, u32[]{:S(2)}) collective-permute-start(bf16[192,256]{1,0:T(8,128)(2,1)S(1)} %collective-permute-done.38), channel_id=1, source_target_pairs={{0,28},{4,0},{8,4},{12,8},{16,12},{20,16},{24,20},{28,24},{1,29},{... | collective-permute-start | bytes 294920 | tf_op jit(solution)/shard_map/ppermute | solution.py:24
  (31 other events, 204.2 us)
Sparse Core Ops, SparseCore 0:
  65.4 21.0 reduce-scatter.6
  122.2 19.4 reduce-scatter.8
  177.5 19.4 reduce-scatter.10
  233.0 19.3 reduce-scatter.12
  288.4 19.4 reduce-scatter.14
  342.8 18.0 reduce-scatter.16
